TPU v7x, 32 devices: a whole 2x2x4 slice. The times are simulated.
32 devices in a mesh: outer: 4 (over x, core), rep: 2 (over y), fsdp: 4 (over z).
Axes of the slice: x: 2, y: 2, z: 4, core: 2. Of those that a mesh axis runs over, the one named last changes fastest.
Arguments:
- deltas: bfloat16 [8, 2304, 18432], P(('outer', 'rep'), None, 'fsdp'), may hold values from -0.119628906 to 0.119628906
- master: float32 [2304, 18432], P(('outer', 'rep'), 'fsdp'), may hold values from -0.125 to 0.125
- momentum: float32 [2304, 18432], P(('outer', 'rep'), 'fsdp'), may hold values from -0.06 to 0.06
- tokens: bfloat16 [8, 48, 2304], P(('outer', 'rep'), 'fsdp'), may hold values from -6 to 6
Outputs:
- new_master: float32 [2304, 18432], P(('outer', 'rep'), 'fsdp')
- hidden: bfloat16 [8, 48, 18432], P(('outer', 'rep'), None, 'fsdp')
All inputs are finite; a program needn't handle non-finite values.
Results may differ from a plain program's by a relative error of at most 0.01.
Values may be sent and summed in bfloat16 or wider, within the bound.
A program may use at most 128 MiB of HBM per device.

v0:
```python
import functools

import jax
import jax.numpy as jnp
from jax import lax
from jax.experimental import pallas as pl
from jax.experimental.pallas import tpu as pltpu
from jax.sharding import PartitionSpec as P

outer_rate = 0.7
decay_rate = 0.9
LANES = 128
PACK = 16
MESH = pl.DeviceIdType.MESH


def plain_shards(deltas, master, momentum, tokens):
    outer_count = lax.axis_size("outer")
    rep_count = lax.axis_size("rep")
    terms = deltas[0].astype(jnp.float32)
    whole_tokens = lax.all_gather(tokens, "fsdp", axis=1, tiled=True)[0]
    summed = lax.psum_scatter(
        terms.astype(jnp.bfloat16), ("outer", "rep"), scatter_dimension=0, tiled=True
    ).astype(jnp.float32)
    average = summed / (outer_count * rep_count)
    moment = decay_rate * momentum + average
    new_master = master - outer_rate * (average + decay_rate * moment)
    weights = new_master.astype(jnp.bfloat16)
    product = jnp.dot(
        whole_tokens,
        lax.all_gather(weights, ("outer", "rep"), axis=0, tiled=True),
        preferred_element_type=jnp.float32,
    )
    hidden = jax.nn.gelu(product, approximate=True).astype(jnp.bfloat16)[None]
    return (new_master, hidden)


def f32(v):
    return v.astype(jnp.float32)


class Exchange:
    def __init__(self, given, held, r0, r1, r2, send, recv, at, peers):
        self.given, self.held = given, held
        self.r0, self.r1, self.r2 = r0, r1, r2
        self.send, self.recv = send, recv
        self.x, self.y = at
        self.core, self.peers = peers

    def copy(self, stage, src, dst, piece, peer):
        return pltpu.make_async_remote_copy(
            src_ref=src,
            dst_ref=dst.at[piece],
            send_sem=self.send.at[stage, piece],
            recv_sem=self.recv.at[stage, piece],
            device_id=peer,
            device_id_type=MESH,
        )

    def copy0(self, piece):
        return self.copy(0, self.given(piece), self.r0, piece, self.core)

    def copy1(self, piece, kind):
        if kind == 0:
            src = self.held.at[piece, 1 - self.x]
        else:
            src = self.held.at[piece, :, 1 - self.y]
        return self.copy(1, src, self.r1, piece, self.peers[kind])

    def spot2(self, kind):
        return (self.x, 1 - self.y) if kind == 0 else (1 - self.x, self.y)

    def copy2(self, piece, kind):
        a, b = self.spot2(kind)
        return self.copy(2, self.held.at[piece, a, b], self.r2, piece, self.peers[1 - kind])

    def go1(self, piece, kind):
        self.copy0(piece).wait_recv()
        for k in range(2):
            a, b = (1 - self.x, k) if kind == 0 else (k, 1 - self.y)
            total = f32(self.held[piece, a, b]) + f32(self.r0[piece, a, b])
            self.held[piece, a, b] = total.astype(jnp.bfloat16)
        self.copy1(piece, kind).start()

    def go2(self, piece, kind):
        self.copy1(piece, kind).wait_recv()
        a, b = self.spot2(kind)
        total = f32(self.held[piece, a, b]) + f32(self.r0[piece, a, b])
        total = total + f32(self.r1[piece, b if kind == 0 else a])
        self.held[piece, a, b] = total.astype(jnp.bfloat16)
        self.copy2(piece, kind).start()

    def last(self, piece, kind):
        self.copy2(piece, kind).wait_recv()
        total = f32(self.held[piece, self.x, self.y]) + f32(self.r0[piece, self.x, self.y])
        total = total + f32(self.r1[piece, self.y if kind == 0 else self.x])
        return total + f32(self.r2[piece])

    def sent(self, piece, kind):
        self.copy0(piece).wait_send()
        self.copy1(piece, kind).wait_send()
        self.copy2(piece, kind).wait_send()


def kernel(
    pieces, width, fsdp_count, count, token_rows,
    deltas, master, momentum, tokens, mbuf, hbuf,
    held, d0, d1, d2, part, p0, p1, p2, vbuf, raw, cut, tokf, tokg, packed, lined, tok,
    dsend, drecv, psend, precv, load_sem, state_sem,
    fsend, frecv, gsend, grecv, own_sem,
):
    o, y, f = lax.axis_index("outer"), lax.axis_index("rep"), lax.axis_index("fsdp")
    x, c = o // 2, o % 2
    core_peer = {"outer": x * 2 + 1 - c}
    x_peer = {"outer": (1 - x) * 2 + c}
    y_peer = {"rep": 1 - y}

    def flip(v, bit):
        return 1 - v if bit else v

    others = [(dc, dx, dy) for dc in range(2) for dx in range(2) for dy in range(2)][1:]
    group = [
        ({"outer": flip(x, dx) * 2 + flip(c, dc), "rep": flip(y, dy)},
         (flip(x, dx) * 2 + flip(c, dc)) * 2 + flip(y, dy))
        for dc, dx, dy in others
    ]
    along = [{"fsdp": (f + k) % fsdp_count} for k in range(1, fsdp_count)]

    barrier = pltpu.get_barrier_semaphore()
    for peer in along + [g for g, _ in group]:
        pl.semaphore_signal(barrier, inc=1, device_id=peer, device_id_type=MESH)

    def columns(piece):
        return pl.ds(pl.multiple_of(piece * width, LANES), width)

    sums = Exchange(
        lambda piece: deltas.at[:, 1 - c, :, :, columns(piece)],
        held, d0, d1, d2, dsend, drecv, (x, y), (core_peer, (x_peer, y_peer)),
    )
    prods = Exchange(
        lambda piece: part.at[1 - c, piece],
        part.at[c], p0, p1, p2, psend, precv, (x, y), (core_peer, (x_peer, y_peer)),
    )

    def load(piece):
        return pltpu.make_async_copy(deltas.at[:, c, :, :, columns(piece)], held.at[piece], load_sem.at[piece])

    states = (
        pltpu.make_async_copy(master, mbuf, state_sem.at[0]),
        pltpu.make_async_copy(momentum, vbuf, state_sem.at[1]),
    )
    tok_load = pltpu.make_async_copy(tokens, raw, own_sem.at[2])
    tok_own = pltpu.make_async_copy(cut, tokf.at[f], own_sem.at[0])
    tok_along = [
        pltpu.make_async_remote_copy(
            src_ref=cut, dst_ref=tokf.at[f], send_sem=fsend.at[k], recv_sem=frecv.at[k],
            device_id=peer, device_id_type=MESH,
        )
        for k, peer in enumerate(along)
    ]
    slot = (c * 2 + x) * 2 + y
    tok_keep = pltpu.make_async_copy(lined.at[o * 2 + y], tokg.at[slot], own_sem.at[1])
    tok_group = [
        pltpu.make_async_remote_copy(
            src_ref=lined.at[share], dst_ref=tokg.at[slot], send_sem=gsend.at[k], recv_sem=grecv.at[k],
            device_id=peer, device_id_type=MESH,
        )
        for k, (peer, share) in enumerate(group)
    ]

    def over(body):
        def step(i, carry):
            for kind in range(2):
                body(2 * i + kind, kind)
            return carry

        lax.fori_loop(0, pieces // 2, step, 0)

    def fetch(piece, kind):
        load(piece).start()

    def begin(piece, kind):
        sums.copy0(piece).start()

    def first(piece, kind):
        load(piece).wait()
        sums.go1(piece, kind)

    over(fetch)
    tok_load.start()
    pl.semaphore_wait(barrier, len(along) + len(group))
    over(begin)
    for copy in states:
        copy.start()
    over(first)
    tok_load.wait()
    depth = cut.shape[2]
    cut[...] = jnp.zeros_like(cut)
    for g in range(count):
        cut[g, :token_rows] = f32(raw[...])[:, g * depth:(g + 1) * depth].astype(jnp.bfloat16)
    tok_own.start()
    for copy in tok_along:
        copy.start()

    tok_own.wait()
    for copy in tok_along:
        copy.wait_recv()
    for g in range(count):
        for k in range(fsdp_count):
            packed[g, pl.ds(k * token_rows, token_rows), :] = f32(tokf[k, g])[:token_rows]
    lined[...] = packed[...].astype(jnp.bfloat16)
    tok_keep.start()
    for copy in tok_group:
        copy.start()

    over(sums.go2)

    tok_keep.wait()
    for copy in tok_group:
        copy.wait_recv()
    tok[...] = tokg[...].reshape(tok.shape)
    for copy in states:
        copy.wait()

    def update(piece, kind):
        at = columns(piece)
        average = sums.last(piece, kind) / count
        moment = decay_rate * vbuf[:, at] + average
        fresh = mbuf[:, at] - outer_rate * (average + decay_rate * moment)
        mbuf[:, at] = fresh
        product = jnp.dot(tok[...], fresh.astype(jnp.bfloat16), preferred_element_type=jnp.float32)
        product = product.astype(jnp.bfloat16).reshape((2, 2, 2) + hbuf.shape[:1] + (width,))
        part[0, piece] = product[0]
        part[1, piece] = product[1]
        prods.copy0(piece).start()

    def update_then(piece, kind):
        update(piece, kind)

        @pl.when(piece > 0)
        def _():
            prods.go1(piece - 1, 1 - kind)

    over(update_then)
    prods.go1(pieces - 1, 1)
    over(prods.go2)

    def finish(piece, kind):
        v = prods.last(piece, kind)
        inner = 0.7978845608028654 * (v + 0.044715 * (v * v * v))
        hbuf[:, columns(piece)] = (0.5 * v * (1.0 + jnp.tanh(inner))).astype(jnp.bfloat16)

    over(finish)

    def settle(piece, kind):
        sums.sent(piece, kind)
        prods.sent(piece, kind)

    over(settle)
    for copy in tok_along + tok_group:
        copy.wait_send()


def fast_shards(pieces, deltas, master, momentum, tokens):
    fsdp_count = lax.axis_size("fsdp")
    count = lax.axis_size("outer") * lax.axis_size("rep")
    depth, wide = deltas.shape[1:]
    rows = depth // count
    width = wide // pieces
    token_rows = tokens.shape[1]
    padded = -(-token_rows // PACK) * PACK
    own_tokens = token_rows * fsdp_count
    blocks = deltas.reshape(2, 2, 2, rows, wide)
    half = jnp.bfloat16
    dma = pltpu.SemaphoreType.DMA
    anywhere = pl.BlockSpec(memory_space=pl.ANY)
    new_master, hidden = pl.pallas_call(
        functools.partial(kernel, pieces, width, fsdp_count, count, token_rows),
        out_shape=(
            pltpu.VMEM((rows, wide), jnp.float32),
            pltpu.VMEM((own_tokens, wide), half),
        ),
        in_specs=[anywhere] * 4,
        out_specs=(pl.BlockSpec(memory_space=pltpu.VMEM),) * 2,
        scratch_shapes=[
            pltpu.VMEM((pieces, 2, 2, rows, width), half),
            pltpu.VMEM((pieces, 2, 2, rows, width), half),
            pltpu.VMEM((pieces, 2, rows, width), half),
            pltpu.VMEM((pieces, rows, width), half),
            pltpu.VMEM((2, pieces, 2, 2, own_tokens, width), half),
            pltpu.VMEM((pieces, 2, 2, own_tokens, width), half),
            pltpu.VMEM((pieces, 2, own_tokens, width), half),
            pltpu.VMEM((pieces, own_tokens, width), half),
            pltpu.VMEM((rows, wide), jnp.float32),
            pltpu.VMEM((token_rows, depth), half),
            pltpu.VMEM((count, padded, rows), half),
            pltpu.VMEM((fsdp_count, count, padded, rows), half),
            pltpu.VMEM((count, own_tokens, rows), half),
            pltpu.VMEM((count, own_tokens, rows), jnp.float32),
            pltpu.VMEM((count, own_tokens, rows), half),
            pltpu.VMEM((count * own_tokens, rows), half),
            dma((3, pieces)), dma((3, pieces)), dma((3, pieces)), dma((3, pieces)),
            dma((pieces,)), dma((2,)),
            dma((fsdp_count - 1,)), dma((fsdp_count - 1,)), dma((count - 1,)), dma((count - 1,)), dma((3,)),
        ],
        compiler_params=pltpu.CompilerParams(
            collective_id=0, has_side_effects=True, vmem_limit_bytes=58 * 1024 * 1024
        ),
    )(blocks, master, momentum, tokens[0])
    parts = 8 if rows % 64 == 0 else 4 if rows % 32 == 0 else 1
    return pl.pallas_call(
        functools.partial(write_out, parts),
        out_shape=(
            jax.ShapeDtypeStruct((rows, wide), jnp.float32),
            jax.ShapeDtypeStruct((1, own_tokens, wide), half),
        ),
        in_specs=[pl.BlockSpec(memory_space=pltpu.VMEM)] * 2,
        out_specs=(anywhere, anywhere),
        scratch_shapes=[dma((parts + 1,))],
        compiler_params=pltpu.CompilerParams(vmem_limit_bytes=1024 * 1024),
    )(
        pltpu.with_memory_space_constraint(new_master, pltpu.VMEM),
        pltpu.with_memory_space_constraint(hidden, pltpu.VMEM),
    )


def write_out(parts, fresh, shown, new_master, hidden, sem):
    rows = fresh.shape[0] // parts
    copies = [
        pltpu.make_async_copy(fresh.at[pl.ds(k * rows, rows)], new_master.at[pl.ds(k * rows, rows)], sem.at[k])
        for k in range(parts)
    ]
    copies.append(pltpu.make_async_copy(shown, hidden.at[0], sem.at[parts]))
    for copy in copies:
        copy.start()
    for copy in copies:
        copy.wait()


def pieces_for(mesh, deltas):
    if mesh.shape["outer"] != 4 or mesh.shape["rep"] != 2:
        return None
    count = mesh.shape["outer"] * mesh.shape["rep"]
    wide = deltas.shape[2] // mesh.shape["fsdp"]
    if deltas.shape[1] % (count * PACK):
        return None
    for pieces in (18, 16, 12, 10, 8, 6, 4, 2):
        if wide % (pieces * LANES) == 0:
            return pieces
    return None


def solution(mesh):
    in_specs = (
        P(("outer", "rep"), None, "fsdp"),
        P(("outer", "rep"), "fsdp"),
        P(("outer", "rep"), "fsdp"),
        P(("outer", "rep"), "fsdp", None),
    )
    out_specs = (P(("outer", "rep"), "fsdp"), P(("outer", "rep"), None, "fsdp"))

    def run(deltas, master, momentum, tokens):
        pieces = pieces_for(mesh, deltas)
        shards = plain_shards if pieces is None else functools.partial(fast_shards, pieces)
        return jax.shard_map(shards, mesh=mesh, in_specs=in_specs, out_specs=out_specs, check_vma=False)(
            deltas, master, momentum, tokens
        )

    return run
```

profile of v0, /device:TPU:0, one launch (start us, length us, event | category | flops | bytes accessed | tf_op | source)
XLA Modules:
  0.0 118.6 jit_solution(10943992145506238028)
XLA Ops:
  0.6 115.4 %shard_map.59 = (f32[288,4608]{1,0:T(8,128)S(1)}, bf16[48,4608]{1,0:T(8,128)(2,1)S(1)}) custom-call(bf16[2,2,2,288,4608]{4,3,2,1,0:T(8,128)(2,1)} %bitcast.2, f32[288,4608]{1,0:T(8,128)} %master.1, f32[288,4608]{1,0:T(8,128)} %momentum.1, bf16[12,2304]{1,0:T(8,128)(2,1)} %bitcast.3), custom_call_target="tpu_custom_call" | custom-call | tf_op jit(solution)/shard_map/pallas_call | solution.py:277
  116.0 2.6 %shard_map.60 = (f32[288,4608]{1,0:T(8,128)}, bf16[1,48,4608]{2,1,0:T(8,128)(2,1)}) custom-call(f32[288,4608]{1,0:T(8,128)S(1)} %get-tuple-element.4.fresh, bf16[48,4608]{1,0:T(8,128)(2,1)S(1)} %get-tuple-element.5.shown), custom_call_target="tpu_custom_call" | custom-call | tf_op jit(solution)/shard_map/pallas_call | solution.py:311
where the time goes:
time: 119 us
  Pallas kernels  118 us (99%)
    pallas_call x1, Pallas kernels, fast_shards(): pl.pallas_call(functools.partial(kernel, pieces, width, fsdp_count, count...  115 us
    pallas_call x1, Pallas kernels, fast_shards(): pl.pallas_call(functools.partial(write_out, parts), out_shape=(jax.ShapeD...  2.56 us

commit v1 on v0

--- a/solution.py
+++ b/solution.py
@@ -11,6 +11,7 @@
 decay_rate = 0.9
 LANES = 128
 PACK = 16
+AHEAD = 4
 MESH = pl.DeviceIdType.MESH
 
 
@@ -104,10 +105,10 @@
 
 def kernel(
     pieces, width, fsdp_count, count, token_rows,
-    deltas, master, momentum, tokens, mbuf, hbuf,
-    held, d0, d1, d2, part, p0, p1, p2, vbuf, raw, cut, tokf, tokg, packed, lined, tok,
+    deltas, master, momentum, tokens, fresh_out, shown_out,
+    held, d0, d1, d2, part, p0, p1, p2, mbuf, hbuf, vbuf, raw, cut, tokg, tokf, packed, tok,
     dsend, drecv, psend, precv, load_sem, state_sem,
-    fsend, frecv, gsend, grecv, own_sem,
+    fsend, frecv, gsend, grecv, own_sem, fresh_sem, shown_sem,
 ):
     o, y, f = lax.axis_index("outer"), lax.axis_index("rep"), lax.axis_index("fsdp")
     x, c = o // 2, o % 2
@@ -149,24 +150,25 @@
         pltpu.make_async_copy(master, mbuf, state_sem.at[0]),
         pltpu.make_async_copy(momentum, vbuf, state_sem.at[1]),
     )
+    slot = (c * 2 + x) * 2 + y
     tok_load = pltpu.make_async_copy(tokens, raw, own_sem.at[2])
-    tok_own = pltpu.make_async_copy(cut, tokf.at[f], own_sem.at[0])
+    tok_keep = pltpu.make_async_copy(cut.at[o * 2 + y], tokg.at[slot], own_sem.at[1])
+    tok_group = [
+        pltpu.make_async_remote_copy(
+            src_ref=cut.at[share], dst_ref=tokg.at[slot], send_sem=gsend.at[k], recv_sem=grecv.at[k],
+            device_id=peer, device_id_type=MESH,
+        )
+        for k, (peer, share) in enumerate(group)
+    ]
+    tok_own = pltpu.make_async_copy(tokg, tokf.at[f], own_sem.at[0])
     tok_along = [
         pltpu.make_async_remote_copy(
-            src_ref=cut, dst_ref=tokf.at[f], send_sem=fsend.at[k], recv_sem=frecv.at[k],
+            src_ref=tokg, dst_ref=tokf.at[f], send_sem=fsend.at[k], recv_sem=frecv.at[k],
             device_id=peer, device_id_type=MESH,
         )
         for k, peer in enumerate(along)
     ]
-    slot = (c * 2 + x) * 2 + y
-    tok_keep = pltpu.make_async_copy(lined.at[o * 2 + y], tokg.at[slot], own_sem.at[1])
-    tok_group = [
-        pltpu.make_async_remote_copy(
-            src_ref=lined.at[share], dst_ref=tokg.at[slot], send_sem=gsend.at[k], recv_sem=grecv.at[k],
-            device_id=peer, device_id_type=MESH,
-        )
-        for k, (peer, share) in enumerate(group)
-    ]
+    fresh_copy = pltpu.make_async_copy(mbuf, fresh_out, fresh_sem.at[0])
 
     def over(body):
         def step(i, carry):
@@ -179,46 +181,45 @@
     def fetch(piece, kind):
         load(piece).start()
 
-    def begin(piece, kind):
-        sums.copy0(piece).start()
-
     def first(piece, kind):
+        @pl.when(piece + AHEAD < pieces)
+        def _():
+            sums.copy0(piece + AHEAD).start()
+
         load(piece).wait()
         sums.go1(piece, kind)
 
+    tok_load.start()
     over(fetch)
-    tok_load.start()
     pl.semaphore_wait(barrier, len(along) + len(group))
-    over(begin)
-    for copy in states:
-        copy.start()
-    over(first)
+    for piece in range(min(AHEAD, pieces)):
+        sums.copy0(piece).start()
     tok_load.wait()
     depth = cut.shape[2]
     cut[...] = jnp.zeros_like(cut)
     for g in range(count):
         cut[g, :token_rows] = f32(raw[...])[:, g * depth:(g + 1) * depth].astype(jnp.bfloat16)
+    tok_keep.start()
+    for copy in tok_group:
+        copy.start()
+    over(first)
+    for copy in states:
+        copy.start()
+    tok_keep.wait()
+    for copy in tok_group:
+        copy.wait_recv()
     tok_own.start()
     for copy in tok_along:
         copy.start()
-
     tok_own.wait()
     for copy in tok_along:
         copy.wait_recv()
     for g in range(count):
         for k in range(fsdp_count):
             packed[g, pl.ds(k * token_rows, token_rows), :] = f32(tokf[k, g])[:token_rows]
-    lined[...] = packed[...].astype(jnp.bfloat16)
-    tok_keep.start()
-    for copy in tok_group:
-        copy.start()
+    tok[...] = packed[...].astype(jnp.bfloat16).reshape(tok.shape)
 
     over(sums.go2)
-
-    tok_keep.wait()
-    for copy in tok_group:
-        copy.wait_recv()
-    tok[...] = tokg[...].reshape(tok.shape)
     for copy in states:
         copy.wait()
 
@@ -243,20 +244,27 @@
 
     over(update_then)
     prods.go1(pieces - 1, 1)
+    fresh_copy.start()
     over(prods.go2)
+
+    def shown_copy(piece):
+        return pltpu.make_async_copy(hbuf.at[:, columns(piece)], shown_out.at[:, columns(piece)], shown_sem.at[piece])
 
     def finish(piece, kind):
         v = prods.last(piece, kind)
         inner = 0.7978845608028654 * (v + 0.044715 * (v * v * v))
         hbuf[:, columns(piece)] = (0.5 * v * (1.0 + jnp.tanh(inner))).astype(jnp.bfloat16)
+        shown_copy(piece).start()
 
     over(finish)
 
     def settle(piece, kind):
         sums.sent(piece, kind)
         prods.sent(piece, kind)
+        shown_copy(piece).wait()
 
     over(settle)
+    fresh_copy.wait()
     for copy in tok_along + tok_group:
         copy.wait_send()
 
@@ -281,7 +289,7 @@
             pltpu.VMEM((own_tokens, wide), half),
         ),
         in_specs=[anywhere] * 4,
-        out_specs=(pl.BlockSpec(memory_space=pltpu.VMEM),) * 2,
+        out_specs=(anywhere, anywhere),
         scratch_shapes=[
             pltpu.VMEM((pieces, 2, 2, rows, width), half),
             pltpu.VMEM((pieces, 2, 2, rows, width), half),
@@ -292,16 +300,18 @@
             pltpu.VMEM((pieces, 2, own_tokens, width), half),
             pltpu.VMEM((pieces, own_tokens, width), half),
             pltpu.VMEM((rows, wide), jnp.float32),
+            pltpu.VMEM((own_tokens, wide), half),
+            pltpu.VMEM((rows, wide), jnp.float32),
             pltpu.VMEM((token_rows, depth), half),
             pltpu.VMEM((count, padded, rows), half),
+            pltpu.VMEM((count, padded, rows), half),
             pltpu.VMEM((fsdp_count, count, padded, rows), half),
-            pltpu.VMEM((count, own_tokens, rows), half),
             pltpu.VMEM((count, own_tokens, rows), jnp.float32),
-            pltpu.VMEM((count, own_tokens, rows), half),
             pltpu.VMEM((count * own_tokens, rows), half),
             dma((3, pieces)), dma((3, pieces)), dma((3, pieces)), dma((3, pieces)),
             dma((pieces,)), dma((2,)),
             dma((fsdp_count - 1,)), dma((fsdp_count - 1,)), dma((count - 1,)), dma((count - 1,)), dma((3,)),
+            dma((1,)), dma((pieces,)),
         ],
         compiler_params=pltpu.CompilerParams(
             collective_id=0, has_side_effects=True, vmem_limit_bytes=58 * 1024 * 1024

time: 119 us -> 116 us (0.975)
  Pallas kernels: 118 us -> 115 us
    pallas_call x1, Pallas kernels: 115 us -> 112 us  [fast_shards(): pl.pallas_call(functools.partial(kernel, pieces, width, fsdp_count, count...]
where the time goes in v1:
time: 116 us
  Pallas kernels  115 us (99%)
    pallas_call x1, Pallas kernels, fast_shards(): pl.pallas_call(functools.partial(kernel, pieces, width, fsdp_count, count...  112 us
    pallas_call x1, Pallas kernels, fast_shards(): pl.pallas_call(functools.partial(write_out, parts), out_shape=(jax.ShapeD...  2.56 us

profile of v1, /device:TPU:0, one launch (start us, length us, event | category | flops | bytes accessed | tf_op | source)
XLA Modules:
  0.0 115.6 jit_solution(1150965959228040962)
XLA Ops:
  0.6 112.4 %shard_map.59 = (f32[288,4608]{1,0:T(8,128)S(1)}, bf16[48,4608]{1,0:T(8,128)(2,1)S(1)}) custom-call(bf16[2,2,2,288,4608]{4,3,2,1,0:T(8,128)(2,1)} %bitcast.2, f32[288,4608]{1,0:T(8,128)} %master.1, f32[288,4608]{1,0:T(8,128)} %momentum.1, bf16[12,2304]{1,0:T(8,128)(2,1)} %bitcast.3), custom_call_target="tpu_custom_call" | custom-call | tf_op jit(solution)/shard_map/pallas_call | solution.py:285
  113.1 2.6 %shard_map.60 = (f32[288,4608]{1,0:T(8,128)}, bf16[1,48,4608]{2,1,0:T(8,128)(2,1)}) custom-call(f32[288,4608]{1,0:T(8,128)S(1)} %get-tuple-element.4.fresh, bf16[48,4608]{1,0:T(8,128)(2,1)S(1)} %get-tuple-element.5.shown), custom_call_target="tpu_custom_call" | custom-call | tf_op jit(solution)/shard_map/pallas_call | solution.py:321

commit v2 on v1

--- a/solution.py
+++ b/solution.py
@@ -11,7 +11,7 @@
 decay_rate = 0.9
 LANES = 128
 PACK = 16
-AHEAD = 4
+AHEAD = 2
 MESH = pl.DeviceIdType.MESH
 
 
@@ -48,59 +48,57 @@
         self.x, self.y = at
         self.core, self.peers = peers
 
-    def copy(self, stage, src, dst, piece, peer):
+    def copy(self, stage, src, dst, pair, peer):
         return pltpu.make_async_remote_copy(
             src_ref=src,
-            dst_ref=dst.at[piece],
-            send_sem=self.send.at[stage, piece],
-            recv_sem=self.recv.at[stage, piece],
+            dst_ref=dst,
+            send_sem=self.send.at[stage],
+            recv_sem=self.recv.at[stage, pair],
             device_id=peer,
             device_id_type=MESH,
         )
 
-    def copy0(self, piece):
-        return self.copy(0, self.given(piece), self.r0, piece, self.core)
-
-    def copy1(self, piece, kind):
-        if kind == 0:
-            src = self.held.at[piece, 1 - self.x]
-        else:
-            src = self.held.at[piece, :, 1 - self.y]
-        return self.copy(1, src, self.r1, piece, self.peers[kind])
+    def got(self, stage, pair):
+        box = (self.r0, self.r1, self.r2)[stage].at[pl.ds(2 * pair, 2)]
+        self.copy(stage, box, box, pair, self.core).wait_recv()
+
+    def sent(self):
+        for stage, box in enumerate((self.r0, self.r1, self.r2)):
+            self.copy(stage, box, box, 0, self.core).wait_send()
 
     def spot2(self, kind):
         return (self.x, 1 - self.y) if kind == 0 else (1 - self.x, self.y)
 
-    def copy2(self, piece, kind):
-        a, b = self.spot2(kind)
-        return self.copy(2, self.held.at[piece, a, b], self.r2, piece, self.peers[1 - kind])
-
-    def go1(self, piece, kind):
-        self.copy0(piece).wait_recv()
-        for k in range(2):
-            a, b = (1 - self.x, k) if kind == 0 else (k, 1 - self.y)
+    def go0(self, pair):
+        for kind in range(2):
+            piece = 2 * pair + kind
+            self.copy(0, self.given(piece), self.r0.at[piece], pair, self.core).start()
+
+    def go1(self, pair):
+        self.got(0, pair)
+        for kind in range(2):
+            piece = 2 * pair + kind
+            for k in range(2):
+                a, b = (1 - self.x, k) if kind == 0 else (k, 1 - self.y)
+                total = f32(self.held[piece, a, b]) + f32(self.r0[piece, a, b])
+                self.held[piece, a, b] = total.astype(jnp.bfloat16)
+            src = self.held.at[piece, 1 - self.x] if kind == 0 else self.held.at[piece, :, 1 - self.y]
+            self.copy(1, src, self.r1.at[piece], pair, self.peers[kind]).start()
+
+    def go2(self, pair):
+        self.got(1, pair)
+        for kind in range(2):
+            piece = 2 * pair + kind
+            a, b = self.spot2(kind)
             total = f32(self.held[piece, a, b]) + f32(self.r0[piece, a, b])
+            total = total + f32(self.r1[piece, b if kind == 0 else a])
             self.held[piece, a, b] = total.astype(jnp.bfloat16)
-        self.copy1(piece, kind).start()
-
-    def go2(self, piece, kind):
-        self.copy1(piece, kind).wait_recv()
-        a, b = self.spot2(kind)
-        total = f32(self.held[piece, a, b]) + f32(self.r0[piece, a, b])
-        total = total + f32(self.r1[piece, b if kind == 0 else a])
-        self.held[piece, a, b] = total.astype(jnp.bfloat16)
-        self.copy2(piece, kind).start()
+            self.copy(2, self.held.at[piece, a, b], self.r2.at[piece], pair, self.peers[1 - kind]).start()
 
     def last(self, piece, kind):
-        self.copy2(piece, kind).wait_recv()
         total = f32(self.held[piece, self.x, self.y]) + f32(self.r0[piece, self.x, self.y])
         total = total + f32(self.r1[piece, self.y if kind == 0 else self.x])
         return total + f32(self.r2[piece])
-
-    def sent(self, piece, kind):
-        self.copy0(piece).wait_send()
-        self.copy1(piece, kind).wait_send()
-        self.copy2(piece, kind).wait_send()
 
 
 def kernel(
@@ -109,6 +107,7 @@
     held, d0, d1, d2, part, p0, p1, p2, mbuf, hbuf, vbuf, raw, cut, tokg, tokf, packed, tok,
     dsend, drecv, psend, precv, load_sem, state_sem,
     fsend, frecv, gsend, grecv, own_sem, fresh_sem, shown_sem,
+    core_sem, plane_sem, all_sem,
 ):
     o, y, f = lax.axis_index("outer"), lax.axis_index("rep"), lax.axis_index("fsdp")
     x, c = o // 2, o % 2
@@ -127,9 +126,19 @@
     ]
     along = [{"fsdp": (f + k) % fsdp_count} for k in range(1, fsdp_count)]
 
+    corner = x * y
+    lead = corner * c
+
+    def counter(at_x, at_y):
+        return {"outer": at_x * 2 + 1 - at_x * at_y, "rep": at_y}
+
     barrier = pltpu.get_barrier_semaphore()
-    for peer in along + [g for g, _ in group]:
-        pl.semaphore_signal(barrier, inc=1, device_id=peer, device_id_type=MESH)
+    for at_x, at_y in ((1 - x, y), (x, 1 - y), (1 - x, 1 - y)):
+        pl.semaphore_signal(barrier, inc=1, device_id=counter(at_x, at_y), device_id_type=MESH)
+
+    @pl.when(c == 1)
+    def _():
+        pl.semaphore_signal(barrier, inc=1, device_id=core_peer, device_id_type=MESH)
 
     def columns(piece):
         return pl.ds(pl.multiple_of(piece * width, LANES), width)
@@ -143,7 +152,8 @@
         part.at[c], p0, p1, p2, psend, precv, (x, y), (core_peer, (x_peer, y_peer)),
     )
 
-    def load(piece):
+    def load(pair, kind):
+        piece = 2 * pair + kind
         return pltpu.make_async_copy(deltas.at[:, c, :, :, columns(piece)], held.at[piece], load_sem.at[piece])
 
     states = (
@@ -155,65 +165,115 @@
     tok_keep = pltpu.make_async_copy(cut.at[o * 2 + y], tokg.at[slot], own_sem.at[1])
     tok_group = [
         pltpu.make_async_remote_copy(
-            src_ref=cut.at[share], dst_ref=tokg.at[slot], send_sem=gsend.at[k], recv_sem=grecv.at[k],
+            src_ref=cut.at[share], dst_ref=tokg.at[slot], send_sem=gsend.at[0], recv_sem=grecv.at[0],
             device_id=peer, device_id_type=MESH,
         )
-        for k, (peer, share) in enumerate(group)
+        for peer, share in group
     ]
+    group_all = pltpu.make_async_remote_copy(
+        src_ref=cut.at[pl.ds(0, count - 1)], dst_ref=tokg.at[pl.ds(0, count - 1)], send_sem=gsend.at[0],
+        recv_sem=grecv.at[0], device_id=core_peer, device_id_type=MESH,
+    )
     tok_own = pltpu.make_async_copy(tokg, tokf.at[f], own_sem.at[0])
     tok_along = [
         pltpu.make_async_remote_copy(
-            src_ref=tokg, dst_ref=tokf.at[f], send_sem=fsend.at[k], recv_sem=frecv.at[k],
+            src_ref=tokg, dst_ref=tokf.at[f], send_sem=fsend.at[0], recv_sem=frecv.at[0],
             device_id=peer, device_id_type=MESH,
         )
-        for k, peer in enumerate(along)
+        for peer in along
     ]
+    along_box = tokf.at[pl.ds(0, fsdp_count - 1)]
+    along_all = pltpu.make_async_remote_copy(
+        src_ref=along_box, dst_ref=along_box, send_sem=fsend.at[0], recv_sem=frecv.at[0],
+        device_id=core_peer, device_id_type=MESH,
+    )
     fresh_copy = pltpu.make_async_copy(mbuf, fresh_out, fresh_sem.at[0])
 
+    pairs = pieces // 2
+
     def over(body):
-        def step(i, carry):
+        def step(pair, carry):
+            body(pair)
+            return carry
+
+        lax.fori_loop(0, pairs, step, 0)
+
+    def fetch(pair):
+        @pl.when(pair > 0)
+        def _():
             for kind in range(2):
-                body(2 * i + kind, kind)
-            return carry
-
-        lax.fori_loop(0, pieces // 2, step, 0)
-
-    def fetch(piece, kind):
-        load(piece).start()
-
-    def first(piece, kind):
-        @pl.when(piece + AHEAD < pieces)
+                load(pair, kind).start()
+
+    def first(pair):
+        @pl.when(pair + AHEAD < pairs)
         def _():
-            sums.copy0(piece + AHEAD).start()
-
-        load(piece).wait()
-        sums.go1(piece, kind)
+            sums.go0(pair + AHEAD)
+
+        for kind in range(2):
+            load(pair, kind).wait()
+        sums.go1(pair)
 
     tok_load.start()
+    for kind in range(2):
+        load(0, kind).start()
+
+    @pl.when(c == 0)
+    def _():
+        pl.semaphore_wait(barrier, 1 + 6 * corner)
+        pl.semaphore_signal(core_sem, inc=1, device_id=core_peer, device_id_type=MESH)
+
+    @pl.when(c == 1)
+    def _():
+        pl.semaphore_wait(core_sem, 1)
+
+    for pair in range(min(AHEAD, pairs)):
+        sums.go0(pair)
     over(fetch)
-    pl.semaphore_wait(barrier, len(along) + len(group))
-    for piece in range(min(AHEAD, pieces)):
-        sums.copy0(piece).start()
+
+    @pl.when(lead == 1)
+    def _():
+        for peer in along:
+            pl.semaphore_signal(barrier, inc=1, device_id=peer, device_id_type=MESH)
+
     tok_load.wait()
     depth = cut.shape[2]
     cut[...] = jnp.zeros_like(cut)
     for g in range(count):
         cut[g, :token_rows] = f32(raw[...])[:, g * depth:(g + 1) * depth].astype(jnp.bfloat16)
     tok_keep.start()
+
+    @pl.when((c == 1) & (corner == 0))
+    def _():
+        pl.semaphore_wait(barrier, 6)
+        pl.semaphore_signal(plane_sem, inc=1, device_id=core_peer, device_id_type=MESH)
+
+    @pl.when((c == 0) & (corner == 0))
+    def _():
+        pl.semaphore_wait(plane_sem, 1)
+
     for copy in tok_group:
         copy.start()
     over(first)
     for copy in states:
         copy.start()
     tok_keep.wait()
-    for copy in tok_group:
-        copy.wait_recv()
+    group_all.wait_recv()
     tok_own.start()
+
+    @pl.when(lead == 1)
+    def _():
+        pl.semaphore_wait(barrier, len(along))
+        for peer, _ in group:
+            pl.semaphore_signal(all_sem, inc=1, device_id=peer, device_id_type=MESH)
+
+    @pl.when(lead == 0)
+    def _():
+        pl.semaphore_wait(all_sem, 1)
+
     for copy in tok_along:
         copy.start()
     tok_own.wait()
-    for copy in tok_along:
-        copy.wait_recv()
+    along_all.wait_recv()
     for g in range(count):
         for k in range(fsdp_count):
             packed[g, pl.ds(k * token_rows, token_rows), :] = f32(tokf[k, g])[:token_rows]
@@ -223,50 +283,50 @@
     for copy in states:
         copy.wait()
 
-    def update(piece, kind):
-        at = columns(piece)
-        average = sums.last(piece, kind) / count
-        moment = decay_rate * vbuf[:, at] + average
-        fresh = mbuf[:, at] - outer_rate * (average + decay_rate * moment)
-        mbuf[:, at] = fresh
-        product = jnp.dot(tok[...], fresh.astype(jnp.bfloat16), preferred_element_type=jnp.float32)
-        product = product.astype(jnp.bfloat16).reshape((2, 2, 2) + hbuf.shape[:1] + (width,))
-        part[0, piece] = product[0]
-        part[1, piece] = product[1]
-        prods.copy0(piece).start()
-
-    def update_then(piece, kind):
-        update(piece, kind)
-
-        @pl.when(piece > 0)
+    def update(pair):
+        sums.got(2, pair)
+        for kind in range(2):
+            piece = 2 * pair + kind
+            at = columns(piece)
+            average = sums.last(piece, kind) / count
+            moment = decay_rate * vbuf[:, at] + average
+            fresh = mbuf[:, at] - outer_rate * (average + decay_rate * moment)
+            mbuf[:, at] = fresh
+            product = jnp.dot(tok[...], fresh.astype(jnp.bfloat16), preferred_element_type=jnp.float32)
+            product = product.astype(jnp.bfloat16).reshape((2, 2, 2) + hbuf.shape[:1] + (width,))
+            part[0, piece] = product[0]
+            part[1, piece] = product[1]
+        prods.go0(pair)
+
+        @pl.when(pair > 0)
         def _():
-            prods.go1(piece - 1, 1 - kind)
-
-    over(update_then)
-    prods.go1(pieces - 1, 1)
+            prods.go1(pair - 1)
+
+    over(update)
+    prods.go1(pairs - 1)
     fresh_copy.start()
     over(prods.go2)
 
-    def shown_copy(piece):
-        return pltpu.make_async_copy(hbuf.at[:, columns(piece)], shown_out.at[:, columns(piece)], shown_sem.at[piece])
-
-    def finish(piece, kind):
-        v = prods.last(piece, kind)
-        inner = 0.7978845608028654 * (v + 0.044715 * (v * v * v))
-        hbuf[:, columns(piece)] = (0.5 * v * (1.0 + jnp.tanh(inner))).astype(jnp.bfloat16)
-        shown_copy(piece).start()
+    def shown_copy(pair):
+        at = pl.ds(pl.multiple_of(pair * 2 * width, LANES), 2 * width)
+        return pltpu.make_async_copy(hbuf.at[:, at], shown_out.at[:, at], shown_sem.at[0])
+
+    def finish(pair):
+        prods.got(2, pair)
+        for kind in range(2):
+            piece = 2 * pair + kind
+            v = prods.last(piece, kind)
+            inner = 0.7978845608028654 * (v + 0.044715 * (v * v * v))
+            hbuf[:, columns(piece)] = (0.5 * v * (1.0 + jnp.tanh(inner))).astype(jnp.bfloat16)
+        shown_copy(pair).start()
 
     over(finish)
-
-    def settle(piece, kind):
-        sums.sent(piece, kind)
-        prods.sent(piece, kind)
-        shown_copy(piece).wait()
-
-    over(settle)
+    sums.sent()
+    prods.sent()
+    group_all.wait_send()
+    along_all.wait_send()
     fresh_copy.wait()
-    for copy in tok_along + tok_group:
-        copy.wait_send()
+    pltpu.make_async_copy(hbuf, shown_out, shown_sem.at[0]).wait()
 
 
 def fast_shards(pieces, deltas, master, momentum, tokens):
@@ -281,6 +341,7 @@
     blocks = deltas.reshape(2, 2, 2, rows, wide)
     half = jnp.bfloat16
     dma = pltpu.SemaphoreType.DMA
+    regular = pltpu.SemaphoreType.REGULAR
     anywhere = pl.BlockSpec(memory_space=pl.ANY)
     new_master, hidden = pl.pallas_call(
         functools.partial(kernel, pieces, width, fsdp_count, count, token_rows),
@@ -308,10 +369,11 @@
             pltpu.VMEM((fsdp_count, count, padded, rows), half),
             pltpu.VMEM((count, own_tokens, rows), jnp.float32),
             pltpu.VMEM((count * own_tokens, rows), half),
-            dma((3, pieces)), dma((3, pieces)), dma((3, pieces)), dma((3, pieces)),
+            dma((3,)), dma((3, pieces // 2)), dma((3,)), dma((3, pieces // 2)),
             dma((pieces,)), dma((2,)),
-            dma((fsdp_count - 1,)), dma((fsdp_count - 1,)), dma((count - 1,)), dma((count - 1,)), dma((3,)),
-            dma((1,)), dma((pieces,)),
+            dma((1,)), dma((1,)), dma((1,)), dma((1,)), dma((3,)),
+            dma((1,)), dma((1,)),
+            regular, regular, regular,
         ],
         compiler_params=pltpu.CompilerParams(
             collective_id=0, has_side_effects=True, vmem_limit_bytes=58 * 1024 * 1024

time: 116 us -> 111 us (0.957)
  Pallas kernels: 115 us -> 110 us
    pallas_call x1, Pallas kernels: 112 us -> 108 us  [fast_shards(): pl.pallas_call(functools.partial(kernel, pieces, width, fsdp_count, count...]
where the time goes in v2:
time: 111 us
  Pallas kernels  110 us (99%)
    pallas_call x1, Pallas kernels, fast_shards(): pl.pallas_call(functools.partial(kernel, pieces, width, fsdp_count, count...  108 us
    pallas_call x1, Pallas kernels, fast_shards(): pl.pallas_call(functools.partial(write_out, parts), out_shape=(jax.ShapeD...  2.56 us

profile of v2, /device:TPU:0, one launch (start us, length us, event | category | flops | bytes accessed | tf_op | source)
XLA Modules:
  0.0 110.8 jit_solution(18349228462877956720)
XLA Ops:
  0.6 107.6 %shard_map.59 = (f32[288,4608]{1,0:T(8,128)S(1)}, bf16[48,4608]{1,0:T(8,128)(2,1)S(1)}) custom-call(bf16[2,2,2,288,4608]{4,3,2,1,0:T(8,128)(2,1)} %bitcast.2, f32[288,4608]{1,0:T(8,128)} %master.1, f32[288,4608]{1,0:T(8,128)} %momentum.1, bf16[12,2304]{1,0:T(8,128)(2,1)} %bitcast.3), custom_call_target="tpu_custom_call" | custom-call | tf_op jit(solution)/shard_map/pallas_call | solution.py:346
  108.3 2.6 %shard_map.60 = (f32[288,4608]{1,0:T(8,128)}, bf16[1,48,4608]{2,1,0:T(8,128)(2,1)}) custom-call(f32[288,4608]{1,0:T(8,128)S(1)} %get-tuple-element.4.fresh, bf16[48,4608]{1,0:T(8,128)(2,1)S(1)} %get-tuple-element.5.shown), custom_call_target="tpu_custom_call" | custom-call | tf_op jit(solution)/shard_map/pallas_call | solution.py:383

commit v3 on v2

--- a/solution.py
+++ b/solution.py
@@ -12,6 +12,8 @@
 LANES = 128
 PACK = 16
 AHEAD = 2
+HEAD = 3
+LAG = 2
 MESH = pl.DeviceIdType.MESH
 
 
@@ -74,16 +76,36 @@
             piece = 2 * pair + kind
             self.copy(0, self.given(piece), self.r0.at[piece], pair, self.core).start()
 
-    def go1(self, pair):
-        self.got(0, pair)
+    def forward1(self, pair, at):
         for kind in range(2):
             piece = 2 * pair + kind
             for k in range(2):
                 a, b = (1 - self.x, k) if kind == 0 else (k, 1 - self.y)
-                total = f32(self.held[piece, a, b]) + f32(self.r0[piece, a, b])
-                self.held[piece, a, b] = total.astype(jnp.bfloat16)
-            src = self.held.at[piece, 1 - self.x] if kind == 0 else self.held.at[piece, :, 1 - self.y]
-            self.copy(1, src, self.r1.at[piece], pair, self.peers[kind]).start()
+                total = f32(self.held[piece, a, b, at]) + f32(self.r0[piece, a, b, at])
+                self.held[piece, a, b, at] = total.astype(jnp.bfloat16)
+            src = self.held.at[piece, 1 - self.x, :, at] if kind == 0 else self.held.at[piece, :, 1 - self.y, at]
+            self.copy(1, src, self.r1.at[piece, :, at], pair, self.peers[kind]).start()
+
+    def go1(self, pair):
+        self.got(0, pair)
+        self.forward1(pair, pl.ds(0, self.r0.shape[3]))
+
+    def head0(self, cuts, sem):
+        for h, at in enumerate(cuts):
+            for kind in range(2):
+                pltpu.make_async_remote_copy(
+                    src_ref=self.given(kind).at[:, :, at], dst_ref=self.r0.at[kind, :, :, at],
+                    send_sem=self.send.at[0], recv_sem=sem.at[h], device_id=self.core, device_id_type=MESH,
+                ).start()
+
+    def head1(self, cuts, sem):
+        for h, at in enumerate(cuts):
+            box = self.r0.at[pl.ds(0, 2), :, :, at]
+            pltpu.make_async_remote_copy(
+                src_ref=box, dst_ref=box, send_sem=self.send.at[0], recv_sem=sem.at[h],
+                device_id=self.core, device_id_type=MESH,
+            ).wait_recv()
+            self.forward1(0, at)
 
     def go2(self, pair):
         self.got(1, pair)
@@ -105,7 +127,7 @@
     pieces, width, fsdp_count, count, token_rows,
     deltas, master, momentum, tokens, fresh_out, shown_out,
     held, d0, d1, d2, part, p0, p1, p2, mbuf, hbuf, vbuf, raw, cut, tokg, tokf, packed, tok,
-    dsend, drecv, psend, precv, load_sem, state_sem,
+    dsend, drecv, psend, precv, load_sem, state_sem, head_sem,
     fsend, frecv, gsend, grecv, own_sem, fresh_sem, shown_sem,
     core_sem, plane_sem, all_sem,
 ):
@@ -152,9 +174,9 @@
         part.at[c], p0, p1, p2, psend, precv, (x, y), (core_peer, (x_peer, y_peer)),
     )
 
-    def load(pair, kind):
+    def load(pair, kind, which):
         piece = 2 * pair + kind
-        return pltpu.make_async_copy(deltas.at[:, c, :, :, columns(piece)], held.at[piece], load_sem.at[piece])
+        return pltpu.make_async_copy(deltas.at[:, c, :, :, columns(piece)], held.at[piece], load_sem.at[which])
 
     states = (
         pltpu.make_async_copy(master, mbuf, state_sem.at[0]),
@@ -191,31 +213,47 @@
 
     pairs = pieces // 2
 
-    def over(body):
+    def over(body, start=0, stop=pairs):
         def step(pair, carry):
             body(pair)
             return carry
 
-        lax.fori_loop(0, pairs, step, 0)
+        lax.fori_loop(start, stop, step, 0)
+
+    rows = held.shape[3]
+    step = rows // (HEAD * PACK) * PACK
+    cuts = [pl.ds(h * step, step if h < HEAD - 1 else rows - h * step) for h in range(HEAD)] if step else [pl.ds(0, rows)]
+
+    def held_wait(start, size, which):
+        box = held.at[pl.ds(start, size)]
+        pltpu.make_async_copy(box, box, load_sem.at[which]).wait()
 
     def fetch(pair):
         @pl.when(pair > 0)
         def _():
             for kind in range(2):
-                load(pair, kind).start()
+                load(pair, kind, 1).start()
 
     def first(pair):
         @pl.when(pair + AHEAD < pairs)
         def _():
             sums.go0(pair + AHEAD)
 
-        for kind in range(2):
-            load(pair, kind).wait()
-        sums.go1(pair)
+        @pl.when(pair == 1)
+        def _():
+            held_wait(2, pieces - 2, 1)
+
+        @pl.when(pair > 0)
+        def _():
+            sums.go1(pair)
+
+        @pl.when(pair >= LAG)
+        def _():
+            sums.go2(pair - LAG)
 
     tok_load.start()
     for kind in range(2):
-        load(0, kind).start()
+        load(0, kind, 0).start()
 
     @pl.when(c == 0)
     def _():
@@ -226,7 +264,8 @@
     def _():
         pl.semaphore_wait(core_sem, 1)
 
-    for pair in range(min(AHEAD, pairs)):
+    sums.head0(cuts, head_sem)
+    for pair in range(1, min(AHEAD, pairs)):
         sums.go0(pair)
     over(fetch)
 
@@ -253,7 +292,10 @@
 
     for copy in tok_group:
         copy.start()
-    over(first)
+    held_wait(0, 2, 0)
+    sums.head1(cuts, head_sem)
+    lag = min(LAG, pairs)
+    over(first, 0, lag)
     for copy in states:
         copy.start()
     tok_keep.wait()
@@ -272,6 +314,7 @@
 
     for copy in tok_along:
         copy.start()
+    over(first, lag, pairs)
     tok_own.wait()
     along_all.wait_recv()
     for g in range(count):
@@ -279,7 +322,7 @@
             packed[g, pl.ds(k * token_rows, token_rows), :] = f32(tokf[k, g])[:token_rows]
     tok[...] = packed[...].astype(jnp.bfloat16).reshape(tok.shape)
 
-    over(sums.go2)
+    over(sums.go2, pairs - lag, pairs)
     for copy in states:
         copy.wait()
 
@@ -370,7 +413,7 @@
             pltpu.VMEM((count, own_tokens, rows), jnp.float32),
             pltpu.VMEM((count * own_tokens, rows), half),
             dma((3,)), dma((3, pieces // 2)), dma((3,)), dma((3, pieces // 2)),
-            dma((pieces,)), dma((2,)),
+            dma((2,)), dma((2,)), dma((HEAD,)),
             dma((1,)), dma((1,)), dma((1,)), dma((1,)), dma((3,)),
             dma((1,)), dma((1,)),
             regular, regular, regular,

time: 111 us -> 110 us (level)
  no operation moved by 1% of the time
where the time goes in v3:
time: 110 us
  Pallas kernels  110 us (100%)
    pallas_call x1, Pallas kernels, fast_shards(): pl.pallas_call(functools.partial(kernel, pieces, width, fsdp_count, count...  107 us
    pallas_call x1, Pallas kernels, fast_shards(): pl.pallas_call(functools.partial(write_out, parts), out_shape=(jax.ShapeD...  2.56 us

profile of v3, /device:TPU:0, one launch (start us, length us, event | category | flops | bytes accessed | tf_op | source)
XLA Modules:
  0.0 110.3 jit_solution(1136180430047739260)
XLA Ops:
  0.6 107.1 %shard_map.59 = (f32[288,4608]{1,0:T(8,128)S(1)}, bf16[48,4608]{1,0:T(8,128)(2,1)S(1)}) custom-call(bf16[2,2,2,288,4608]{4,3,2,1,0:T(8,128)(2,1)} %bitcast.2, f32[288,4608]{1,0:T(8,128)} %master.1, f32[288,4608]{1,0:T(8,128)} %momentum.1, bf16[12,2304]{1,0:T(8,128)(2,1)} %bitcast.3), custom_call_target="tpu_custom_call" | custom-call | tf_op jit(solution)/shard_map/pallas_call | solution.py:389
  107.7 2.6 %shard_map.60 = (f32[288,4608]{1,0:T(8,128)}, bf16[1,48,4608]{2,1,0:T(8,128)(2,1)}) custom-call(f32[288,4608]{1,0:T(8,128)S(1)} %get-tuple-element.4.fresh, bf16[48,4608]{1,0:T(8,128)(2,1)S(1)} %get-tuple-element.5.shown), custom_call_target="tpu_custom_call" | custom-call | tf_op jit(solution)/shard_map/pallas_call | solution.py:426

commit v4 on v3

--- a/solution.py
+++ b/solution.py
@@ -11,9 +11,9 @@
 decay_rate = 0.9
 LANES = 128
 PACK = 16
-AHEAD = 2
-HEAD = 3
-LAG = 2
+AHEAD = 1
+HEAD = 6
+LAG = 6
 MESH = pl.DeviceIdType.MESH
 
 
@@ -125,10 +125,10 @@
 
 def kernel(
     pieces, width, fsdp_count, count, token_rows,
-    deltas, master, momentum, tokens, fresh_out, shown_out,
-    held, d0, d1, d2, part, p0, p1, p2, mbuf, hbuf, vbuf, raw, cut, tokg, tokf, packed, tok,
+    deltas, master, momentum, tokens, mbuf, hbuf,
+    held, d0, d1, d2, part, p0, p1, p2, vbuf, raw, cut, tokg, tokf, packed, tok,
     dsend, drecv, psend, precv, load_sem, state_sem, head_sem,
-    fsend, frecv, gsend, grecv, own_sem, fresh_sem, shown_sem,
+    fsend, frecv, gsend, grecv, own_sem,
     core_sem, plane_sem, all_sem,
 ):
     o, y, f = lax.axis_index("outer"), lax.axis_index("rep"), lax.axis_index("fsdp")
@@ -209,7 +209,6 @@
         src_ref=along_box, dst_ref=along_box, send_sem=fsend.at[0], recv_sem=frecv.at[0],
         device_id=core_peer, device_id_type=MESH,
     )
-    fresh_copy = pltpu.make_async_copy(mbuf, fresh_out, fresh_sem.at[0])
 
     pairs = pieces // 2
 
@@ -347,12 +346,7 @@
 
     over(update)
     prods.go1(pairs - 1)
-    fresh_copy.start()
     over(prods.go2)
-
-    def shown_copy(pair):
-        at = pl.ds(pl.multiple_of(pair * 2 * width, LANES), 2 * width)
-        return pltpu.make_async_copy(hbuf.at[:, at], shown_out.at[:, at], shown_sem.at[0])
 
     def finish(pair):
         prods.got(2, pair)
@@ -361,15 +355,12 @@
             v = prods.last(piece, kind)
             inner = 0.7978845608028654 * (v + 0.044715 * (v * v * v))
             hbuf[:, columns(piece)] = (0.5 * v * (1.0 + jnp.tanh(inner))).astype(jnp.bfloat16)
-        shown_copy(pair).start()
 
     over(finish)
     sums.sent()
     prods.sent()
     group_all.wait_send()
     along_all.wait_send()
-    fresh_copy.wait()
-    pltpu.make_async_copy(hbuf, shown_out, shown_sem.at[0]).wait()
 
 
 def fast_shards(pieces, deltas, master, momentum, tokens):
@@ -393,7 +384,7 @@
             pltpu.VMEM((own_tokens, wide), half),
         ),
         in_specs=[anywhere] * 4,
-        out_specs=(anywhere, anywhere),
+        out_specs=(pl.BlockSpec(memory_space=pltpu.VMEM),) * 2,
         scratch_shapes=[
             pltpu.VMEM((pieces, 2, 2, rows, width), half),
             pltpu.VMEM((pieces, 2, 2, rows, width), half),
@@ -404,8 +395,6 @@
             pltpu.VMEM((pieces, 2, own_tokens, width), half),
             pltpu.VMEM((pieces, own_tokens, width), half),
             pltpu.VMEM((rows, wide), jnp.float32),
-            pltpu.VMEM((own_tokens, wide), half),
-            pltpu.VMEM((rows, wide), jnp.float32),
             pltpu.VMEM((token_rows, depth), half),
             pltpu.VMEM((count, padded, rows), half),
             pltpu.VMEM((count, padded, rows), half),
@@ -415,7 +404,6 @@
             dma((3,)), dma((3, pieces // 2)), dma((3,)), dma((3, pieces // 2)),
             dma((2,)), dma((2,)), dma((HEAD,)),
             dma((1,)), dma((1,)), dma((1,)), dma((1,)), dma((3,)),
-            dma((1,)), dma((1,)),
             regular, regular, regular,
         ],
         compiler_params=pltpu.CompilerParams(
@@ -459,7 +447,7 @@
     wide = deltas.shape[2] // mesh.shape["fsdp"]
     if deltas.shape[1] % (count * PACK):
         return None
-    for pieces in (18, 16, 12, 10, 8, 6, 4, 2):
+    for pieces in (12, 18, 16, 10, 8, 6, 4, 2):
         if wide % (pieces * LANES) == 0:
             return pieces
     return None

time: 110 us -> 110 us (level)
  no operation moved by 1% of the time
where the time goes in v4:
time: 110 us
  Pallas kernels  109 us (99%)
    pallas_call x1, Pallas kernels, fast_shards(): pl.pallas_call(functools.partial(kernel, pieces, width, fsdp_count, count...  107 us
    pallas_call x1, Pallas kernels, fast_shards(): pl.pallas_call(functools.partial(write_out, parts), out_shape=(jax.ShapeD...  2.56 us

profile of v4, /device:TPU:0, one launch (start us, length us, event | category | flops | bytes accessed | tf_op | source)
XLA Modules:
  0.0 110.0 jit_solution(7781551570346835668)
XLA Ops:
  0.6 106.8 %shard_map.59 = (f32[288,4608]{1,0:T(8,128)S(1)}, bf16[48,4608]{1,0:T(8,128)(2,1)S(1)}) custom-call(bf16[2,2,2,288,4608]{4,3,2,1,0:T(8,128)(2,1)} %bitcast.2, f32[288,4608]{1,0:T(8,128)} %master.1, f32[288,4608]{1,0:T(8,128)} %momentum.1, bf16[12,2304]{1,0:T(8,128)(2,1)} %bitcast.3), custom_call_target="tpu_custom_call" | custom-call | tf_op jit(solution)/shard_map/pallas_call | solution.py:380
  107.4 2.6 %shard_map.60 = (f32[288,4608]{1,0:T(8,128)}, bf16[1,48,4608]{2,1,0:T(8,128)(2,1)}) custom-call(f32[288,4608]{1,0:T(8,128)S(1)} %get-tuple-element.4.fresh, bf16[48,4608]{1,0:T(8,128)(2,1)S(1)} %get-tuple-element.5.shown), custom_call_target="tpu_custom_call" | custom-call | tf_op jit(solution)/shard_map/pallas_call | solution.py:414
